TPU v7x, 32 devices: a whole 2x2x4 slice. The times are simulated.
32 devices in a mesh: dp: 4 (over x, core), fsdp: 2 (over y), enc: 4 (over z).
Axes of the slice: x: 2, y: 2, z: 4, core: 2. Of those that a mesh axis runs over, the one named last changes fastest.
Arguments:
- hidden: bfloat16 [8192, 8192], P(('dp', 'fsdp', 'enc')), may hold values from -40 to 40
- residual_gradient: bfloat16 [8192, 8192], P(('dp', 'fsdp', 'enc')), may hold values from -3 to 3
- value_output_gradient: bfloat16 [8192, 1024], P(('dp', 'fsdp', 'enc')), may hold values from -6 to 6
- attention_norm_gain: float32 [8192], replicated, may hold values from 0.1 to 1.9
- value_frozen_weight: bfloat16 [8192, 1024], P('fsdp'), may hold values from -0.0625 to 0.0625
- value_down_factor: bfloat16 [8192, 16], replicated, may hold values from -0.0625 to 0.0625
- value_up_factor: bfloat16 [16, 1024], replicated, may hold values from -0.29882812 to 0.29882812
- merger_frozen_weight: bfloat16 [5120, 8192], P(None, ('fsdp', 'enc')), may hold values from -0.078125 to 0.078125
- merger_down_factor: bfloat16 [5120, 16], replicated, may hold values from -0.078125 to 0.078125
- merger_up_factor: bfloat16 [16, 8192], P(None, ('fsdp', 'enc')), may hold values from -0.29882812 to 0.29882812
- merger_saved_preactivation: bfloat16 [1024, 5120], P(('dp', 'fsdp', 'enc')), may hold values from -5 to 5
- image_token_counts: int32 [32], P('dp'), may hold values from 8 to 16, as said below
- image_encoder_owner: int32 [32], P('dp'), may hold values from 0 to 7, as said below
- image_first_rows: int32 [32], P(('dp', 'fsdp', 'enc')), may hold values from 0 to 255, as said below
Outputs:
- layer_input_gradient: bfloat16 [8192, 8192], P(('dp', 'fsdp', 'enc'))
- preactivation_gradient: bfloat16 [1024, 5120], P(('dp', 'fsdp', 'enc'))
- value_down_gradient: float32 [8192, 16], replicated
- value_up_gradient: float32 [16, 1024], replicated
- merger_down_gradient: float32 [5120, 16], replicated
- merger_up_gradient: float32 [16, 8192], P(None, ('fsdp', 'enc'))
Inputs may be any that keep to these rules, and one draw needn't show every extreme that they name: `image_token_counts`: within each data replica some encoder device owns exactly 2 images, all of 16 visual tokens, so its rows fill all 32; no other device owns more than 2 images. `image_encoder_owner`: encoder devices are numbered within the data replica in mesh order. `image_first_rows`: images of one device lie inside its 256 rows in increasing order and don't intersect.
All inputs are finite; a program needn't handle non-finite values.
Results may differ from a plain program's by a relative error of at most 0.0085.
Values may be sent and summed in bfloat16 or wider, within the bound.
No kernel may reach another device: no remote copies, remote signals or barrier semaphores. Data moves between devices by JAX's collectives and lax.ppermute only.
A program may use at most 192 MiB of HBM per device.

v0:
```python
import jax
import jax.numpy as jnp
from jax import lax
from jax.sharding import PartitionSpec as P

MAXIMG = 16
adapter_scale = 2.0
norm_eps = 1e-06


def gelu_parts(preact):
    normal_cdf = 0.5 * (1.0 + lax.erf(preact * 0.7071067811865476))
    normal_pdf = jnp.exp(-0.5 * preact * preact) * 0.3989422804014327
    return (normal_cdf, normal_pdf)


def owner_layout(image_token_counts, image_encoder_owner, owner_count, owner_room, slot_len):
    total_images = image_token_counts.shape[0]
    image_ids = jnp.arange(total_images)
    same_owner = image_encoder_owner[:, None] == image_encoder_owner[None, :]
    earlier = image_ids[None, :] < image_ids[:, None]
    starts = jnp.sum(jnp.where(same_owner & earlier, image_token_counts[None, :], 0), axis=1)
    row_index = jnp.arange(owner_count * owner_room)
    row_owner = row_index // owner_room
    row_place = row_index % owner_room
    matches = (
        (row_owner[:, None] == image_encoder_owner[None, :])
        & (row_place[:, None] >= starts[None, :])
        & (row_place[:, None] < (starts + image_token_counts)[None, :])
    )
    source = jnp.sum(
        jnp.where(matches, image_ids[None, :] * slot_len + row_place[:, None] - starts[None, :], 0),
        axis=1,
    )
    valid_rows = jnp.any(matches, axis=1)
    return (source, valid_rows)


def take_slots(layer_input_gradient, counts_in, offsets_in):
    padded = jnp.concatenate(
        [
            layer_input_gradient,
            jnp.zeros((MAXIMG, layer_input_gradient.shape[1]), layer_input_gradient.dtype),
        ],
        axis=0,
    )
    window = lax.dynamic_slice_in_dim(padded, offsets_in[0], MAXIMG, 0)
    inside = jnp.arange(MAXIMG) < counts_in[0]
    pieces = jnp.where(inside[:, None], window, jnp.zeros_like(window))
    return pieces


def decoder_layer_block(
    incoming_rows,
    residual_input,
    value_incoming,
    attention_norm_gain,
    passed_gradient,
    value_down_factor,
    value_up_factor,
):
    values = incoming_rows.astype(jnp.float32)
    inverse = lax.rsqrt(jnp.mean(values * values, axis=1, keepdims=True) + norm_eps)
    normalized_input = (values * inverse * attention_norm_gain).astype(jnp.bfloat16)
    value_low_product = jnp.dot(
        value_incoming, value_up_factor.T, preferred_element_type=jnp.float32
    ).astype(jnp.bfloat16)
    normalized_gradient = passed_gradient.astype(jnp.float32) + adapter_scale * jnp.dot(
        value_low_product, value_down_factor.T, preferred_element_type=jnp.float32
    )
    gained = attention_norm_gain * normalized_gradient
    layer_input_gradient = (
        residual_input.astype(jnp.float32)
        + inverse * gained
        - values * inverse**3 * jnp.mean(values * gained, axis=1, keepdims=True)
    ).astype(jnp.bfloat16)
    projected_rows = jnp.dot(
        normalized_input, value_down_factor, preferred_element_type=jnp.float32
    ).astype(jnp.bfloat16)
    up_term = lax.dot_general(
        projected_rows, value_incoming, (((0,), (0,)), ((), ())), preferred_element_type=jnp.float32
    )
    down_term = lax.dot_general(
        normalized_input,
        value_low_product,
        (((0,), (0,)), ((), ())),
        preferred_element_type=jnp.float32,
    )
    return (layer_input_gradient, down_term, up_term)


def body(
    hidden,
    residual_gradient,
    value_output_gradient,
    attention_norm_gain,
    value_frozen_weight,
    value_down_factor,
    value_up_factor,
    merger_frozen_weight,
    merger_down_factor,
    merger_up_factor,
    merger_saved_preactivation,
    image_token_counts,
    image_encoder_owner,
    image_first_rows,
):
    device_total = lax.axis_size("dp") * lax.axis_size("fsdp") * lax.axis_size("enc")
    gradient_scale = 256.0 / (hidden.shape[0] * device_total)
    scale_factor = gradient_scale * adapter_scale
    owner_count = lax.axis_size("fsdp") * lax.axis_size("enc")
    owner_room = merger_saved_preactivation.shape[0]
    preact = merger_saved_preactivation.astype(jnp.float32)
    normal_cdf, normal_pdf = gelu_parts(preact)
    activation = (preact * normal_cdf).astype(jnp.bfloat16)
    act_low = jnp.dot(activation, merger_down_factor, preferred_element_type=jnp.float32).astype(
        jnp.bfloat16
    )
    all_low = lax.all_gather(act_low, ("fsdp", "enc"), axis=0, tiled=True)
    columns = lax.dot_general(
        lax.all_gather(value_output_gradient, "fsdp", axis=0, tiled=True),
        value_frozen_weight,
        (((1,), (1,)), ((), ())),
        preferred_element_type=jnp.float32,
    ).astype(jnp.bfloat16)
    passed_gradient = lax.all_to_all(columns, "fsdp", split_axis=0, concat_axis=1, tiled=True)
    layer_input_gradient, down_term, up_term = decoder_layer_block(
        hidden,
        residual_gradient,
        value_output_gradient,
        attention_norm_gain,
        passed_gradient,
        value_down_factor,
        value_up_factor,
    )
    member = lax.axis_index(("fsdp", "enc"))
    local_images = image_first_rows.shape[0]
    local_counts = lax.dynamic_slice_in_dim(
        image_token_counts, member * local_images, local_images, 0
    )
    slots_out = take_slots(layer_input_gradient, local_counts, image_first_rows)
    received = lax.all_to_all(slots_out, ("fsdp", "enc"), split_axis=1, concat_axis=0, tiled=True)
    source, valid_rows = owner_layout(
        image_token_counts, image_encoder_owner, owner_count, owner_room, MAXIMG
    )
    visual_tokens = jnp.where(
        valid_rows[:, None], jnp.take(received, source, axis=0), jnp.zeros((), received.dtype)
    )
    value_partial_sum = lax.dot_general(
        visual_tokens,
        merger_frozen_weight,
        (((1,), (1,)), ((), ())),
        preferred_element_type=jnp.float32,
    )
    low_part = lax.dot_general(
        visual_tokens,
        merger_up_factor,
        (((1,), (1,)), ((), ())),
        preferred_element_type=jnp.float32,
    )
    value_partial_sum = value_partial_sum + adapter_scale * jnp.dot(
        low_part, merger_down_factor.astype(jnp.float32).T, precision=lax.Precision.HIGHEST
    )
    combined_gradient, low_sum = (
        lax.psum_scatter(value_partial_sum, ("fsdp", "enc"), scatter_dimension=0, tiled=True),
        lax.psum_scatter(low_part, ("fsdp", "enc"), scatter_dimension=0, tiled=True),
    )
    preactivation_gradient = (combined_gradient * (normal_cdf + preact * normal_pdf)).astype(
        jnp.bfloat16
    )
    term_a2 = lax.dot_general(
        activation,
        low_sum.astype(jnp.bfloat16),
        (((0,), (0,)), ((), ())),
        preferred_element_type=jnp.float32,
    )
    term_b2 = lax.dot_general(
        all_low, visual_tokens, (((0,), (0,)), ((), ())), preferred_element_type=jnp.float32
    )
    merger_up_gradient = lax.psum(scale_factor * term_b2, "dp")
    value_down_gradient, value_up_gradient, merger_down_gradient = lax.psum(
        (scale_factor * down_term, scale_factor * up_term, scale_factor * term_a2),
        ("dp", "fsdp", "enc"),
    )
    return (
        layer_input_gradient,
        preactivation_gradient,
        value_down_gradient,
        value_up_gradient,
        merger_down_gradient,
        merger_up_gradient,
    )


def solution(mesh):
    placed = (
        P(("dp", "fsdp", "enc"), None),
        P(("dp", "fsdp", "enc"), None),
        P(("dp", "fsdp", "enc"), None),
        P(),
        P("fsdp", None),
        P(),
        P(),
        P(None, ("fsdp", "enc")),
        P(),
        P(None, ("fsdp", "enc")),
        P(("dp", "fsdp", "enc"), None),
        P("dp"),
        P("dp"),
        P(("dp", "fsdp", "enc")),
    )
    return jax.shard_map(
        body,
        mesh=mesh,
        in_specs=placed,
        out_specs=(
            P(("dp", "fsdp", "enc"), None),
            P(("dp", "fsdp", "enc"), None),
            P(),
            P(),
            P(),
            P(None, ("fsdp", "enc")),
        ),
        check_vma=False,
    )
```

profile of v0, /device:TPU:0, one launch (start us, length us, event | category | flops | bytes accessed | tf_op | source)
XLA Modules:
  0.0 520.8 jit_solution(2232127266080886779)
XLA Ops:
  7.2 0.7 all-gather.3.cloned.1.call-update
  7.9 25.7 %all-gather.3.cloned.1.call-done = bf16[512,1024]{1,0:T(8,128)(2,1)} async-done(((bf16[256,1024]{1,0:T(8,128)(2,1)}), bf16[512,1024]{1,0:T(8,128)(2,1)}) %all-gather.3.cloned.1.call-update) | async-done | bytes 1048592 | tf_op jit(solution)/shard_map/all_gather | solution.py:121
  33.6 10.3 %convolution_convert_fusion = bf16[512,4096]{1,0:T(8,128)(2,1)} fusion(bf16[512,1024]{1,0:T(8,128)(2,1)} %all-gather.3.cloned.1.call-done, bf16[4096,1024]{1,0:T(8,128)(2,1)} %param.18), kind=kOutput, calls=%fused_computation.19 | convolution fusion | flops 4297064448 | bytes 13631488 | tf_op jit(solution)/shard_map/dot_general | solution.py:120
  43.9 5.7 %all-to-all-start = ((bf16[2,256,4096]{2,1,0:T(8,128)(2,1)}), bf16[2,256,4096]{2,1,0:T(8,128)(2,1)}, u32[]{:S(2)}, u32[]{:S(2)}) async-start(bf16[2,256,4096]{2,1,0:T(8,128)(2,1)} %bitcast.45), calls=%async_computation | async-start | bytes 8388608 | tf_op jit(solution)/shard_map/all_to_all | solution.py:126
  50.3 0.6 dynamic_slice.6
  50.9 0.2 select_reduce_fusion.1
  51.1 0.7 iota_compare_fusion.1
  51.7 0.1 select_reduce_fusion
  51.9 0.2 convolution_convert_fusion.1
  52.1 45.0 %all-to-all-done = bf16[2,256,4096]{2,1,0:T(8,128)(2,1)} async-done(((bf16[2,256,4096]{2,1,0:T(8,128)(2,1)}), bf16[2,256,4096]{2,1,0:T(8,128)(2,1)}, u32[]{:S(2)}, u32[]{:S(2)}) %all-to-all-start) | async-done | bytes 4194336 | tf_op jit(solution)/shard_map/all_to_all | solution.py:126
  97.1 3.3 convert_bitcast_fusion
  100.4 1.0 copy.34
  101.4 1.2 copy-done.1
  102.6 2.9 fusion.2
  105.5 3.5 fusion.5
  109.0 2.0 copy-done.2
  111.0 0.1 fusion.28
  111.2 0.7 copy.36
  111.9 4.6 all-to-all-start.1
  116.5 0.2 reduce-scatter.7.cloned.1.call-start
  116.7 0.1 fusion.33
  116.8 8.6 %all-to-all-done.1 = bf16[16,8,1024]{2,0,1:T(8,128)(2,1)S(1)} async-done(((bf16[16,8,1024]{2,0,1:T(8,128)(2,1)}), bf16[16,8,1024]{2,0,1:T(8,128)(2,1)S(1)}, u32[]{:S(2)}, u32[]{:S(2)}) %all-to-all-start.1) | async-done | bytes 262176 | tf_op jit(solution)/shard_map/all_to_all | solution.py:142
  125.4 1.2 gather_fusion
  126.6 0.1 select_select_fusion
  126.8 0.2 fusion.38
  127.0 12.6 %fusion.37 = f32[256,5120]{1,0:T(8,128)} fusion(bf16[256,1024]{1,0:T(8,128)(2,1)S(1)} %select_select_fusion, bf16[5120,1024]{1,0:T(8,128)(2,1)} %param.21), kind=kOutput, calls=%fused_computation.69 | convolution fusion | flops 2684354560 | bytes 16252928 | tf_op jit(solution)/shard_map/dot_general | solution.py:149
  139.6 0.8 copy.31
  140.4 0.0 reduce-scatter.5.cloned.1.call-start
  140.5 7.2 %fusion.9 = f32[256,5120]{1,0:T(8,128)} fusion(f32[256,5120]{1,0:T(8,128)} %fusion.37, f32[256,16]{0,1:T(8,128)S(1)} %fusion.38, bf16[5120,16]{0,1:T(8,128)(2,1)S(1)} %copy-done.6), kind=kOutput, calls=%fused_computation.18 | convolution fusion | flops 254279680 | bytes 10665984 | tf_op jit(solution)/shard_map/dot_general | solution.py:161
  147.7 0.0 all-reduce.5.cloned.1.call-start
  147.7 4.2 convolution_multiply_fusion.1
  151.9 4.4 convolution_multiply_fusion.5
  156.3 43.3 %reduce-scatter.7.cloned.1.call-done = f32[32,16]{1,0:T(8,128)} async-done(((f32[256,16]{1,0:T(8,128)}), f32[32,16]{1,0:T(8,128)}) %reduce-scatter.7.cloned.1.call-update) | async-done | bytes 2064
  199.6 0.8 copy.32
  200.4 104.9 %reduce-scatter.5.cloned.1.call-done = f32[32,5120]{1,0:T(8,128)} async-done(((f32[256,5120]{1,0:T(8,128)}), f32[32,5120]{1,0:T(8,128)}) %reduce-scatter.5.cloned.1.call-update) | async-done | bytes 655376 | tf_op jit(solution)/shard_map/reduce_scatter | solution.py:165
  305.3 2.1 fusion.26
  307.4 0.2 fusion.18
  307.6 30.6 %all-gather = bf16[8,32,16]{1,2,0:T(8,128)(2,1)S(1)} all-gather(bf16[1,32,16]{1,2,0:T(8,128)(2,1)S(1)} %fusion.18), channel_id=1, replica_groups=mesh['dp'=4,'fsdp'=2,'enc'=4] {'fsdp','enc'}, dimensions={0}, use_global_device_ids=true | all-gather | bytes 9216 | tf_op jit(solution)/shard_map/all_gather | solution.py:119
  338.2 0.1 reshape.104
  338.3 0.8 convolution_multiply_fusion.4
  339.2 0.0 all-reduce.7.cloned.1.call-start
  339.2 0.9 convolution_multiply_fusion.3
  340.2 30.3 %all-reduce.5.cloned.1.call-done = f32[16,1024]{1,0:T(8,128)} async-done(((f32[16,1024]{1,0:T(8,128)}), f32[16,1024]{1,0:T(8,128)}) %all-reduce.5.cloned.1.call-update) | async-done | bytes 65552 | tf_op jit(solution)/shard_map/psum | solution.py:180
  370.5 137.3 %all-reduce.7.cloned.1.call-done = (f32[8192,16]{0,1:T(8,128)}, f32[16,1024]{1,0:T(8,128)}, f32[5120,16]{0,1:T(8,128)}) async-done(((f32[8192,16]{0,1:T(8,128)}, f32[16,1024]{1,0:T(8,128)}, f32[5120,16]{0,1:T(8,128)}), (f32[8192,16]{0,1:T(8,128)}, f32[16,1024]{1,0:T(8,128)}, f32[5120,16]{0,1:T(8,128)})) %all-reduce.7.cloned.1.call-update) | async-done | bytes 917520 | tf_op jit(solution)/shard_map/psum | solution.py:181
  507.7 1.9 copy.42
  509.6 1.5 copy.43
  511.1 1.7 copy.44
  512.8 1.5 copy.45
  (35 shorter events, 0.2 us)
Async XLA Ops:
  7.2 94.2 %copy-start = (bf16[8192,16]{0,1:T(8,128)(2,1)S(1)}, bf16[8192,16]{0,1:T(8,128)(2,1)}, u32[]{:S(2)}) copy-start(bf16[8192,16]{0,1:T(8,128)(2,1)} %param.19) | copy-start | bytes 786436
  7.2 26.4 %all-gather.3.cloned.1.call-start = ((), (), s32[]{:S(2)}) async-start(), calls=%async_computation.4 | async-start | bytes 1572864 | tf_op jit(solution)/shard_map/all_gather | solution.py:121
  43.8 6.4 %copy-start.11 = (s32[8]{0:T(128)S(1)}, s32[8]{0:T(128)}, u32[]{:S(2)}) copy-start(s32[8]{0:T(128)} %param.25) | copy-start | bytes 100
  43.9 7.0 %copy-start.10 = (s32[8]{0:T(128)S(1)}, s32[8]{0:T(128)}, u32[]{:S(2)}) copy-start(s32[8]{0:T(128)} %param.26) | copy-start | bytes 100
  43.9 8.0 %copy-start.5 = (bf16[256,1024]{1,0:T(8,128)(2,1)S(1)}, bf16[256,1024]{1,0:T(8,128)(2,1)}, u32[]{:S(2)}) copy-start(bf16[256,1024]{1,0:T(8,128)(2,1)} %param.16) | copy-start | bytes 1572868
  43.9 8.0 %copy-start.8 = (bf16[16,1024]{1,0:T(8,128)(2,1)S(1)}, bf16[16,1024]{1,0:T(8,128)(2,1)}, u32[]{:S(2)}) copy-start(bf16[16,1024]{1,0:T(8,128)(2,1)} %param.20) | copy-start | bytes 98308
  43.9 53.3 %all-to-all-start = ((bf16[2,256,4096]{2,1,0:T(8,128)(2,1)}), bf16[2,256,4096]{2,1,0:T(8,128)(2,1)}, u32[]{:S(2)}, u32[]{:S(2)}) async-start(bf16[2,256,4096]{2,1,0:T(8,128)(2,1)} %bitcast.45), calls=%async_computation | async-start | bytes 8388608 | tf_op jit(solution)/shard_map/all_to_all | solution.py:126
  100.4 2.2 copy-start.1
  100.4 2.2 copy-start.7
  102.6 2.9 copy-start.3
  109.0 2.0 copy-start.2
  111.0 15.7 %copy-start.9 = (bf16[16,1024]{1,0:T(8,128)(2,1)S(1)}, bf16[16,1024]{1,0:T(8,128)(2,1)}, u32[]{:S(2)}) copy-start(bf16[16,1024]{1,0:T(8,128)(2,1)} %param.23) | copy-start | bytes 98308
  111.9 13.6 %all-to-all-start.1 = ((bf16[16,8,1024]{2,0,1:T(8,128)(2,1)}), bf16[16,8,1024]{2,0,1:T(8,128)(2,1)S(1)}, u32[]{:S(2)}, u32[]{:S(2)}) async-start(bf16[16,8,1024]{2,0,1:T(8,128)(2,1)} %bitcast.39), calls=%async_computation.1 | async-start | bytes 524288 | tf_op jit(solution)/shard_map/all_to_all | solution.py:142
  116.5 83.1 %reduce-scatter.7.cloned.1.call-start = ((), (), s32[]{:S(2)}) async-start(), calls=%async_computation.7 | async-start | bytes 147456
  127.0 13.4 %copy-start.6 = (bf16[5120,16]{0,1:T(8,128)(2,1)S(1)}, bf16[5120,16]{0,1:T(8,128)(2,1)}, u32[]{:S(2)}) copy-start(bf16[5120,16]{0,1:T(8,128)(2,1)} %param.22) | copy-start | bytes 491524
  140.4 164.9 %reduce-scatter.5.cloned.1.call-start = ((), (), s32[]{:S(2)}) async-start(), calls=%async_computation.5 | async-start | bytes 5898240 | tf_op jit(solution)/shard_map/reduce_scatter | solution.py:165
  147.7 157.6 %copy-start.4 = (bf16[32,5120]{1,0:T(8,128)(2,1)S(1)}, bf16[32,5120]{1,0:T(8,128)(2,1)}, u32[]{:S(2)}) copy-start(bf16[32,5120]{1,0:T(8,128)(2,1)} %param.24) | copy-start | bytes 983044
  147.7 222.8 %all-reduce.5.cloned.1.call-start = ((), (), s32[]{:S(2)}) async-start(), calls=%async_computation.6 | async-start | bytes 131072 | tf_op jit(solution)/shard_map/psum | solution.py:180
  339.2 168.6 %all-reduce.7.cloned.1.call-start = ((), (), s32[]{:S(2)}) async-start(), calls=%async_computation.8 | async-start | bytes 1835008 | tf_op jit(solution)/shard_map/psum | solution.py:181
Sparse Core Ops, SparseCore 0:
  9.5 23.9 all-gather.2
  140.5 59.0 reduce-scatter.6
  203.2 102.0 reduce-scatter.4
  339.3 31.1 all-reduce.4
  376.4 131.3 all-reduce.6
where the time goes:
time: 522 us; the launch traced here: 521 us
  waiting for transfers between devices  396 us (76%)
  matrix products  44 us (8%)
  blocking collectives  30.6 us (6%)
  local copies, waits for them, and re-layouts  14.9 us (3%)
  between operations  14.6 us (3%)
  starting transfers between devices  10.7 us (2%)
  other arithmetic  10.2 us (2%)
    psum x1, waiting for transfers between devices, body(): lax.psum((scale_factor * down_term, scale_factor * up_term, scale_factor...  137 us
    reduce_scatter x1, waiting for transfers between devices, body(): lax.psum_scatter(value_partial_sum, ('fsdp', 'enc'), scatter_dimension=0,...  105 us
    all_to_all x1, waiting for transfers between devices, body(): lax.all_to_all(columns, 'fsdp', split_axis=0, concat_axis=1, tiled=True)  45 us
    unnamed x6, waiting for transfers between devices  44.1 us
    all_gather x1, blocking collectives, body(): all_low = lax.all_gather(act_low, ('fsdp', 'enc'), axis=0, tiled=True)  30.6 us
    psum x1, waiting for transfers between devices, body(): merger_up_gradient = lax.psum(scale_factor * term_b2, 'dp')  30.3 us
    all_gather x1, waiting for transfers between devices, body(): lax.all_gather(value_output_gradient, 'fsdp', axis=0, tiled=True)  25.7 us
    dot_general x1, matrix products, body(): lax.dot_general(visual_tokens, merger_frozen_weight, (((1,), (1,)), ((),...  12.6 us
  transfers between devices with their start and end apart: 7, of which 7 were waited for; matrix products, arithmetic and copies ran while one was open for 4% of the time, Pallas kernels for 0%

commit v1 on v0

--- a/solution.py
+++ b/solution.py
@@ -105,6 +105,11 @@
     image_encoder_owner,
     image_first_rows,
 ):
+
+    def columns_measure(vector):
+        formed = lax.all_gather(vector, axis_name="dp").sum(axis=0)
+        return formed
+
     device_total = lax.axis_size("dp") * lax.axis_size("fsdp") * lax.axis_size("enc")
     gradient_scale = 256.0 / (hidden.shape[0] * device_total)
     scale_factor = gradient_scale * adapter_scale
@@ -177,7 +182,7 @@
     term_b2 = lax.dot_general(
         all_low, visual_tokens, (((0,), (0,)), ((), ())), preferred_element_type=jnp.float32
     )
-    merger_up_gradient = lax.psum(scale_factor * term_b2, "dp")
+    merger_up_gradient = columns_measure(scale_factor * term_b2)
     value_down_gradient, value_up_gradient, merger_down_gradient = lax.psum(
         (scale_factor * down_term, scale_factor * up_term, scale_factor * term_a2),
         ("dp", "fsdp", "enc"),

time: 522 us -> 454 us (0.87)
  waiting for transfers between devices: 396 us -> 325 us
  blocking collectives: 30.6 us -> 36.4 us
    psum x1, waiting for transfers between devices: 137 us -> 96.3 us  [body(): lax.psum((scale_factor * down_term, scale_factor * up_term, scale_factor...]
    psum x1 -> x0, waiting for transfers between devices: 30.3 us -> none  [body(): merger_up_gradient = lax.psum(scale_factor * term_b2, 'dp')]
    all_gather x0 -> x1, blocking collectives: none -> 5.77 us  [columns_measure(): formed = lax.all_gather(vector, axis_name='dp').sum(axis=0)]
    unnamed x31 -> x30, local copies, waits for them, and re-layouts: 11.4 us -> 9.92 us
    unnamed x6 -> x5, waiting for transfers between devices: 44.1 us -> 44.1 us
  transfers between devices with their start and end apart: 7 -> 6, of which waited for: 7 -> 6; matrix products, arithmetic and copies ran while one was open for 4% -> 4% of each run, Pallas kernels for 0% -> 0%
where the time goes in v1:
time: 454 us
  waiting for transfers between devices  325 us (72%)
  matrix products  43.3 us (10%)
  blocking collectives  36.4 us (8%)
  between operations  14.6 us (3%)
  local copies, waits for them, and re-layouts  13.4 us (3%)
  other arithmetic  10.8 us (2%)
  starting transfers between devices  10.7 us (2%)
    reduce_scatter x1, waiting for transfers between devices, body(): lax.psum_scatter(value_partial_sum, ('fsdp', 'enc'), scatter_dimension=0,...  105 us
    psum x1, waiting for transfers between devices, body(): lax.psum((scale_factor * down_term, scale_factor * up_term, scale_factor...  96.3 us
    all_to_all x1, waiting for transfers between devices, body(): lax.all_to_all(columns, 'fsdp', split_axis=0, concat_axis=1, tiled=True)  45 us
    unnamed x5, waiting for transfers between devices  44.1 us
    all_gather x1, blocking collectives, body(): all_low = lax.all_gather(act_low, ('fsdp', 'enc'), axis=0, tiled=True)  30.7 us
    all_gather x1, waiting for transfers between devices, body(): lax.all_gather(value_output_gradient, 'fsdp', axis=0, tiled=True)  25.7 us
    dot_general x1, matrix products, body(): lax.dot_general(visual_tokens, merger_frozen_weight, (((1,), (1,)), ((),...  12.6 us
    dot_general x1, matrix products, body(): lax.dot_general(lax.all_gather(value_output_gradient, 'fsdp', axis=0, til...  10.3 us
  transfers between devices with their start and end apart: 6, of which 6 were waited for; matrix products, arithmetic and copies ran while one was open for 4% of the time, Pallas kernels for 0%

profile of v1, /device:TPU:0, one launch (start us, length us, event | category | flops | bytes accessed | tf_op | source)
XLA Modules:
  0.0 453.8 jit_solution(10912520534768746710)
XLA Ops:
  7.2 0.0 all-gather.4.cloned.1.call-start
  7.2 0.7 all-gather.4.cloned.1.call-update
  7.9 25.7 %all-gather.4.cloned.1.call-done = bf16[512,1024]{1,0:T(8,128)(2,1)} async-done(((bf16[256,1024]{1,0:T(8,128)(2,1)}), bf16[512,1024]{1,0:T(8,128)(2,1)}) %all-gather.4.cloned.1.call-update) | async-done | bytes 1048592 | tf_op jit(solution)/shard_map/all_gather | solution.py:126
  33.6 10.3 %convolution_convert_fusion = bf16[512,4096]{1,0:T(8,128)(2,1)} fusion(bf16[512,1024]{1,0:T(8,128)(2,1)} %all-gather.4.cloned.1.call-done, bf16[4096,1024]{1,0:T(8,128)(2,1)} %param.18), kind=kOutput, calls=%fused_computation.19 | convolution fusion | flops 4297064448 | bytes 13631488 | tf_op jit(solution)/shard_map/dot_general | solution.py:125
  43.9 5.8 %all-to-all-start = ((bf16[2,256,4096]{2,1,0:T(8,128)(2,1)}), bf16[2,256,4096]{2,1,0:T(8,128)(2,1)}, u32[]{:S(2)}, u32[]{:S(2)}) async-start(bf16[2,256,4096]{2,1,0:T(8,128)(2,1)} %bitcast.46), calls=%async_computation | async-start | bytes 8388608 | tf_op jit(solution)/shard_map/all_to_all | solution.py:131
  50.3 0.6 dynamic_slice.6
  50.9 0.2 select_reduce_fusion.1
  51.1 0.7 iota_compare_fusion.1
  51.8 0.1 select_reduce_fusion
  51.9 0.2 convolution_convert_fusion.1
  52.1 45.0 %all-to-all-done = bf16[2,256,4096]{2,1,0:T(8,128)(2,1)} async-done(((bf16[2,256,4096]{2,1,0:T(8,128)(2,1)}), bf16[2,256,4096]{2,1,0:T(8,128)(2,1)}, u32[]{:S(2)}, u32[]{:S(2)}) %all-to-all-start) | async-done | bytes 4194336 | tf_op jit(solution)/shard_map/all_to_all | solution.py:131
  97.1 3.3 convert_bitcast_fusion
  100.4 1.0 copy.34
  101.4 1.2 copy-done.1
  102.6 2.9 fusion.2
  105.5 3.5 fusion.5
  109.0 2.0 copy-done.2
  111.0 0.1 fusion.28
  111.2 0.7 copy.36
  111.9 4.6 %all-to-all-start.1 = ((bf16[16,8,1024]{2,0,1:T(8,128)(2,1)}), bf16[16,8,1024]{2,0,1:T(8,128)(2,1)S(1)}, u32[]{:S(2)}, u32[]{:S(2)}) async-start(bf16[16,8,1024]{2,0,1:T(8,128)(2,1)} %bitcast.40), calls=%async_computation.1 | async-start | bytes 524288 | tf_op jit(solution)/shard_map/all_to_all | solution.py:147
  116.5 0.2 reduce-scatter.7.cloned.1.call-start
  116.8 0.1 fusion.33
  116.9 8.6 %all-to-all-done.1 = bf16[16,8,1024]{2,0,1:T(8,128)(2,1)S(1)} async-done(((bf16[16,8,1024]{2,0,1:T(8,128)(2,1)}), bf16[16,8,1024]{2,0,1:T(8,128)(2,1)S(1)}, u32[]{:S(2)}, u32[]{:S(2)}) %all-to-all-start.1) | async-done | bytes 262176 | tf_op jit(solution)/shard_map/all_to_all | solution.py:147
  125.5 1.2 gather_fusion
  126.6 0.1 select_select_fusion
  126.8 0.2 fusion.38
  127.0 12.6 %fusion.37 = f32[256,5120]{1,0:T(8,128)} fusion(bf16[256,1024]{1,0:T(8,128)(2,1)S(1)} %select_select_fusion, bf16[5120,1024]{1,0:T(8,128)(2,1)} %param.21), kind=kOutput, calls=%fused_computation.69 | convolution fusion | flops 2684354560 | bytes 16252928 | tf_op jit(solution)/shard_map/dot_general | solution.py:154
  139.6 0.8 copy.31
  140.4 0.0 reduce-scatter.5.cloned.1.call-start
  140.5 7.2 %fusion.9 = f32[256,5120]{1,0:T(8,128)} fusion(f32[256,5120]{1,0:T(8,128)} %fusion.37, f32[256,16]{0,1:T(8,128)S(1)} %fusion.38, bf16[5120,16]{0,1:T(8,128)(2,1)S(1)} %copy-done.6), kind=kOutput, calls=%fused_computation.18 | convolution fusion | flops 254279680 | bytes 10665984 | tf_op jit(solution)/shard_map/dot_general | solution.py:166
  147.7 0.0 all-reduce.4.cloned.1.call-start
  147.7 4.2 convolution_multiply_fusion.1
  151.9 4.4 convolution_multiply_fusion.5
  156.3 43.4 %reduce-scatter.7.cloned.1.call-done = f32[32,16]{1,0:T(8,128)} async-done(((f32[256,16]{1,0:T(8,128)}), f32[32,16]{1,0:T(8,128)}) %reduce-scatter.7.cloned.1.call-update) | async-done | bytes 2064
  199.7 0.8 copy.32
  200.5 104.9 %reduce-scatter.5.cloned.1.call-done = f32[32,5120]{1,0:T(8,128)} async-done(((f32[256,5120]{1,0:T(8,128)}), f32[32,5120]{1,0:T(8,128)}) %reduce-scatter.5.cloned.1.call-update) | async-done | bytes 655376 | tf_op jit(solution)/shard_map/reduce_scatter | solution.py:170
  305.3 2.1 fusion.26
  307.4 0.9 convolution_multiply_fusion.3
  308.4 0.2 fusion.18
  308.6 30.7 %all-gather.1 = bf16[8,32,16]{1,2,0:T(8,128)(2,1)S(1)} all-gather(bf16[1,32,16]{1,2,0:T(8,128)(2,1)S(1)} %fusion.18), channel_id=1, replica_groups=mesh['dp'=4,'fsdp'=2,'enc'=4] {'fsdp','enc'}, dimensions={0}, use_global_device_ids=true | all-gather | bytes 9216 | tf_op jit(solution)/shard_map/all_gather | solution.py:124
  339.3 0.1 reshape.105
  339.4 0.2 convolution_multiply_fusion.4
  339.5 5.8 %all-gather = f32[64,1024]{1,0:T(8,128)S(1)} all-gather(f32[16,1024]{1,0:T(8,128)S(1)} %convolution_multiply_fusion.4), channel_id=2, replica_groups=mesh['dp'=4,'fsdp'=2,'enc'=4] {'dp'}, dimensions={0}, use_global_device_ids=true | all-gather | bytes 327680 | tf_op jit(solution)/shard_map/all_gather | solution.py:110
  345.3 0.6 reduce_sum.52
  345.9 96.3 %all-reduce.4.cloned.1.call-done = (f32[8192,16]{0,1:T(8,128)}, f32[16,1024]{1,0:T(8,128)}, f32[5120,16]{0,1:T(8,128)}) async-done(((f32[8192,16]{0,1:T(8,128)}, f32[16,1024]{1,0:T(8,128)}, f32[5120,16]{0,1:T(8,128)}), (f32[8192,16]{0,1:T(8,128)}, f32[16,1024]{1,0:T(8,128)}, f32[5120,16]{0,1:T(8,128)})) %all-reduce.4.cloned.1.call-update) | async-done | bytes 917520 | tf_op jit(solution)/shard_map/psum | solution.py:186
  442.2 1.9 copy.41
  444.1 1.5 copy.42
  445.5 1.7 copy.43
  (33 shorter events, 0.2 us)
Async XLA Ops:
  7.2 94.2 %copy-start = (bf16[8192,16]{0,1:T(8,128)(2,1)S(1)}, bf16[8192,16]{0,1:T(8,128)(2,1)}, u32[]{:S(2)}) copy-start(bf16[8192,16]{0,1:T(8,128)(2,1)} %param.19) | copy-start | bytes 786436
  7.2 26.4 %all-gather.4.cloned.1.call-start = ((), (), s32[]{:S(2)}) async-start(), calls=%async_computation.4 | async-start | bytes 1572864 | tf_op jit(solution)/shard_map/all_gather | solution.py:126
  43.8 6.4 %copy-start.11 = (s32[8]{0:T(128)S(1)}, s32[8]{0:T(128)}, u32[]{:S(2)}) copy-start(s32[8]{0:T(128)} %param.25) | copy-start | bytes 100
  43.8 7.0 %copy-start.10 = (s32[8]{0:T(128)S(1)}, s32[8]{0:T(128)}, u32[]{:S(2)}) copy-start(s32[8]{0:T(128)} %param.26) | copy-start | bytes 100
  43.8 8.0 %copy-start.5 = (bf16[256,1024]{1,0:T(8,128)(2,1)S(1)}, bf16[256,1024]{1,0:T(8,128)(2,1)}, u32[]{:S(2)}) copy-start(bf16[256,1024]{1,0:T(8,128)(2,1)} %param.16) | copy-start | bytes 1572868
  43.9 8.0 %copy-start.8 = (bf16[16,1024]{1,0:T(8,128)(2,1)S(1)}, bf16[16,1024]{1,0:T(8,128)(2,1)}, u32[]{:S(2)}) copy-start(bf16[16,1024]{1,0:T(8,128)(2,1)} %param.20) | copy-start | bytes 98308
  43.9 53.3 %all-to-all-start = ((bf16[2,256,4096]{2,1,0:T(8,128)(2,1)}), bf16[2,256,4096]{2,1,0:T(8,128)(2,1)}, u32[]{:S(2)}, u32[]{:S(2)}) async-start(bf16[2,256,4096]{2,1,0:T(8,128)(2,1)} %bitcast.46), calls=%async_computation | async-start | bytes 8388608 | tf_op jit(solution)/shard_map/all_to_all | solution.py:131
  100.4 2.2 copy-start.1
  100.4 2.2 copy-start.7
  102.6 2.9 copy-start.3
  109.0 2.0 copy-start.2
  111.0 15.7 %copy-start.9 = (bf16[16,1024]{1,0:T(8,128)(2,1)S(1)}, bf16[16,1024]{1,0:T(8,128)(2,1)}, u32[]{:S(2)}) copy-start(bf16[16,1024]{1,0:T(8,128)(2,1)} %param.23) | copy-start | bytes 98308
  111.9 13.6 %all-to-all-start.1 = ((bf16[16,8,1024]{2,0,1:T(8,128)(2,1)}), bf16[16,8,1024]{2,0,1:T(8,128)(2,1)S(1)}, u32[]{:S(2)}, u32[]{:S(2)}) async-start(bf16[16,8,1024]{2,0,1:T(8,128)(2,1)} %bitcast.40), calls=%async_computation.1 | async-start | bytes 524288 | tf_op jit(solution)/shard_map/all_to_all | solution.py:147
  116.5 83.2 %reduce-scatter.7.cloned.1.call-start = ((), (), s32[]{:S(2)}) async-start(), calls=%async_computation.6 | async-start | bytes 147456
  127.0 13.4 %copy-start.6 = (bf16[5120,16]{0,1:T(8,128)(2,1)S(1)}, bf16[5120,16]{0,1:T(8,128)(2,1)}, u32[]{:S(2)}) copy-start(bf16[5120,16]{0,1:T(8,128)(2,1)} %param.22) | copy-start | bytes 491524
  140.4 164.9 %reduce-scatter.5.cloned.1.call-start = ((), (), s32[]{:S(2)}) async-start(), calls=%async_computation.5 | async-start | bytes 5898240 | tf_op jit(solution)/shard_map/reduce_scatter | solution.py:170
  147.7 157.7 %copy-start.4 = (bf16[32,5120]{1,0:T(8,128)(2,1)S(1)}, bf16[32,5120]{1,0:T(8,128)(2,1)}, u32[]{:S(2)}) copy-start(bf16[32,5120]{1,0:T(8,128)(2,1)} %param.24) | copy-start | bytes 983044
  147.7 294.5 %all-reduce.4.cloned.1.call-start = ((), (), s32[]{:S(2)}) async-start(), calls=%async_computation.7 | async-start | bytes 1835008 | tf_op jit(solution)/shard_map/psum | solution.py:186
Sparse Core Ops, SparseCore 0:
  9.5 23.9 all-gather.3
  140.5 59.0 reduce-scatter.6
  203.3 102.0 reduce-scatter.4
  311.2 130.9 all-reduce.3
